TPU v7x, 32 devices: a whole 2x2x4 slice. The times are simulated.
32 devices in a mesh: win: 2 (over y), tmpl: 4 (over z), sta: 4 (over x, core).
Axes of the slice: x: 2, y: 2, z: 4, core: 2. Of those that a mesh axis runs over, the one named last changes fastest.
Arguments:
- records: bfloat16 [384, 3, 3584], P(('win', 'sta')), parts along dimension 0
- templates: bfloat16 [16, 192, 3, 100], P(('win', 'tmpl'), 'sta'), parts along dimension 0
- channel_valid: int32 [16, 192, 3], P(('win', 'tmpl'), 'sta'), parts along dimension 0, may hold values from 0 to 1, as said below
- shifts: int32 [16, 192], P(('win', 'tmpl'), 'sta'), parts along dimension 0, may hold values from 0 to 412, as said below
- hypo_id: int32 [16], P(('win', 'tmpl')), parts along dimension 0, may hold values from 0 to 255
- hypo_xyz: float32 [3, 256], replicated, may hold values from -1 to 1
Outputs:
- peak_score: float32 [6144], P(('win', 'sta')), parts along dimension 0
- evidence: float32 [6144], P(('win', 'sta')), parts along dimension 0
- location: float32 [3, 6144], P(None, ('win', 'sta')), parts along dimension 1
There are 2 independent parts, one for each index of `win`. A program takes and returns all parts, laid end to end along the dimension named above; an argument that names none is the same for every part. Nothing has to cross between parts.
Inputs may be any that keep to these rules, and one draw needn't show every extreme that they name: `channel_valid`: every template has all three channels of at least one station valid. `shifts`: for every template some station has moveout 0.
All inputs are finite; a program needn't handle non-finite values.
Results may differ from a plain program's by a relative error of at most 0.0044.
Values sent between devices are 32-bit elements; how exact they have to be, the bound alone decides.
No kernel may reach another device: no remote copies, remote signals or barrier semaphores. Data moves between devices by JAX's collectives and lax.ppermute only.
A program may use at most 64 MiB of HBM per device.

v0:
```python
import math

import jax
import jax.numpy as jnp
from jax import lax
from jax.sharding import PartitionSpec as P

SAMPLES = 3072


sharpness = 400.0
epsilon = 1e-06


def normed_templates(templates):
    wide = templates.astype(jnp.float32)
    power = jnp.mean(wide * wide, axis=-1, keepdims=True)
    return (wide / (wide.shape[-1] * jnp.sqrt(power + epsilon))).astype(jnp.bfloat16)


def window_norm(channels, taps_len):
    squares = channels.astype(jnp.float32) * channels.astype(jnp.float32)
    ones_kernel = jnp.ones((squares.shape[0], 1, taps_len), jnp.float32)
    energy = lax.conv_general_dilated(
        squares[None],
        ones_kernel,
        (1,),
        "VALID",
        dimension_numbers=("NCH", "OIH", "NCH"),
        feature_group_count=squares.shape[0],
        precision=lax.Precision.HIGHEST,
    )[0]
    return jnp.sqrt(energy / taps_len + epsilon)


def block_trace(records_blk, normed_blk, valid_blk, shift_blk, out_length):
    sta_count, comp_count, in_length = records_blk.shape
    tpl_count, taps_len = (normed_blk.shape[0], normed_blk.shape[-1])
    chan_count = sta_count * comp_count
    channels = records_blk.reshape(chan_count, in_length)
    kernel = jnp.transpose(normed_blk, (1, 2, 0, 3)).reshape(chan_count * tpl_count, 1, taps_len)
    raw_corr = lax.conv_general_dilated(
        channels[None],
        kernel,
        (1,),
        "VALID",
        dimension_numbers=("NCH", "OIH", "NCH"),
        feature_group_count=chan_count,
        preferred_element_type=jnp.float32,
    )[0]
    norms = window_norm(channels, taps_len)
    weights = jnp.transpose(valid_blk, (1, 2, 0)).reshape(chan_count, tpl_count).astype(jnp.float32)
    scaled = raw_corr.reshape(chan_count, tpl_count, -1) / norms[:, None, :] * weights[:, :, None]
    station_sum = jnp.sum(scaled.reshape(sta_count, comp_count, tpl_count, -1), axis=1)

    def align(row, offset):
        return lax.dynamic_slice_in_dim(row, offset, out_length)

    aligned = jax.vmap(jax.vmap(align))(station_sum, shift_blk.T)
    return jnp.sum(aligned, axis=0)


def correlate(records, normed, channel_valid, shifts, out_length):
    sta_total = records.shape[0]
    block_size = math.gcd(sta_total, 8)

    def accumulate(totals, block_index):
        first_row = block_index * block_size
        part_records = lax.dynamic_slice_in_dim(records, first_row, block_size, 0)
        part_normed = lax.dynamic_slice_in_dim(normed, first_row, block_size, 1)
        part_valid = lax.dynamic_slice_in_dim(channel_valid, first_row, block_size, 1)
        part_shift = lax.dynamic_slice_in_dim(shifts, first_row, block_size, 1)
        return (
            totals + block_trace(part_records, part_normed, part_valid, part_shift, out_length),
            None,
        )

    start_value = jnp.zeros((normed.shape[0], out_length), jnp.float32)
    totals, unused = lax.scan(
        accumulate, start_value, jnp.arange(sta_total // block_size, dtype=jnp.int32)
    )
    return totals


def local_stats(traces, counts, hypo_id, hypo_xyz):
    scores = sharpness * (traces / counts[:, None])
    best_local = jnp.max(scores, axis=0)
    weights = jnp.exp(scores - best_local[None, :])
    totals = jnp.sum(weights, axis=0)
    onehot = (hypo_id[:, None] == jnp.arange(hypo_xyz.shape[1], dtype=jnp.int32)[None, :]).astype(
        jnp.float32
    )
    positions = jnp.dot(hypo_xyz, onehot.T, precision=lax.Precision.HIGHEST)
    located = jnp.dot(positions, weights, precision=lax.Precision.HIGHEST)
    return (best_local, totals, located)


def on_device(records, templates, channel_valid, shifts, hypo_id, hypo_xyz):
    normed = normed_templates(templates)
    partial_value = correlate(records, normed, channel_valid, shifts, SAMPLES)
    own_count = jnp.sum(channel_valid, axis=(1, 2)).astype(jnp.float32)
    share_len = SAMPLES // lax.axis_size("sta")
    traces, counts = lax.psum((partial_value, own_count), "sta")
    best_local, totals, located = local_stats(traces, counts, hypo_id, hypo_xyz)
    best = lax.pmax(best_local, "tmpl")
    rescale = jnp.exp(best_local - best)
    totals, located = lax.psum((totals * rescale, located * rescale[None, :]), "tmpl")
    evidence = best + jnp.log(totals)
    location = located / totals[None, :]
    offset = lax.axis_index("sta") * share_len
    best = lax.dynamic_slice_in_dim(best, offset, share_len, 0)
    evidence = lax.dynamic_slice_in_dim(evidence, offset, share_len, 0)
    location = lax.dynamic_slice_in_dim(location, offset, share_len, 1)
    return (best, evidence, location)


def solution(mesh):
    return jax.shard_map(
        on_device,
        mesh=mesh,
        in_specs=(
            P(("win", "sta"), None, None),
            P(("win", "tmpl"), "sta", None, None),
            P(("win", "tmpl"), "sta", None),
            P(("win", "tmpl"), "sta"),
            P(("win", "tmpl")),
            P(),
        ),
        out_specs=(P(("win", "sta")), P(("win", "sta")), P(None, ("win", "sta"))),
        check_vma=False,
    )
```

profile of v0, /device:TPU:0, one launch (start us, length us, event | category | flops | bytes accessed | tf_op | source)
XLA Modules:
  0.0 563.1 jit_solution(18340451828419083034)
XLA Ops:
  3.6 508.1 %while.15 = (s32[]{:T(128)}, f32[2,3072]{1,0:T(2,128)S(1)}, s32[6]{0:T(128)S(1)}, bf16[48,3,3584]{2,0,1:T(8,128)(2,1)}, bf16[2,48,3,100]{3,0,2,1:T(2,128)(2,1)},...) while((s32[]{:T(128)}, f32[2,3072]{1,0:T(2,128)S(1)}, ...), condition=%wide.region_4.5_spmd.clone, body=%wide.region_1.4_spmd.clone.sunk | while | flops 931252096 | bytes 17382444 | solution.py:79
  7.8 9.8 %convolution_select_fusion.2 = f32[8,448,48]{2,0,1:T(8,128)S(1)} fusion(bf16[24,1,7,99]{0,2,3,1:T(8,128)(2,1)S(1)} %slice.39, bf16[24,1,8,448]{0,2,3,1:T(8,128)(2,1)} %copy-done.1, pred[8,448]{0,1:T(8,128)(4,1)S(1)} %bitcast.61, s32[48]{0:T(128)S(1)} %copy-done.7, bf16[48,100]{0,1:T(8,128)(2,1)S(1)} %copy.96), kind=kOutput, calls=%fused_computation.9.clone.1 | convolution fusion | flops 826786176 | bytes 906800 | tf_op jit(solution)/shard_map/while/body/eval_jaxpr/conv_general_dilated | solution.py:42
  20.5 15.7 %fusion.53 = f32[8,448,24]{2,0,1:T(8,128)} fusion(f32[24,1,7,99]{0,2,3,1:T(8,128)S(1)} %slice.40, f32[24,1,8,448]{0,2,3,1:T(8,128)S(1)} %copy.99), kind=kOutput, calls=%fused_computation.4.clone.1 | convolution fusion | flops 103534272 | bytes 754656 | tf_op jit(solution)/shard_map/while/body/eval_jaxpr/conv_general_dilated | solution.py:24
  36.2 2.1 copy.100
  40.2 47.8 %while.16 = (s32[]{:T(128)}, f32[8,2,3485]{2,1,0:T(2,128)S(1)}, s32[16,3]{0,1:T(4,128)S(1)}, f32[16,3072]{1,0:T(8,128)S(1)}, s32[]{:T(128)}, /*index=5*/s32[]{:T(128)}) while((s32[]{:T(128)}, f32[8,2,3485]{2,1,0:T(2,128)S(1)}, s32[16,3]{0,1:T(4,128)S(1)}, f32[16,3072]{1,0:T(8,128)S(1)}, s32[]{:T(128)}, /*index=5*/s32[]{:T(128)}) %tuple.55), condition=%wide.while_cond, body=%wide.while_body.sunk | while | flops 2 | bytes 49289 | solution.py:57
  40.9 2.0 dynamic-slice_bitcast_fusion.2
  43.9 2.0 dynamic-slice_bitcast_fusion.2
  46.9 2.0 dynamic-slice_bitcast_fusion.2
  52.9 2.0 dynamic-slice_bitcast_fusion.2
  55.9 2.0 dynamic-slice_bitcast_fusion.2
  61.8 2.0 dynamic-slice_bitcast_fusion.2
  64.8 2.0 dynamic-slice_bitcast_fusion.2
  67.8 2.0 dynamic-slice_bitcast_fusion.2
  73.8 2.0 dynamic-slice_bitcast_fusion.2
  76.8 2.0 dynamic-slice_bitcast_fusion.2
  79.8 2.0 dynamic-slice_bitcast_fusion.2
  85.7 2.0 dynamic-slice_bitcast_fusion.2
  92.5 9.8 %convolution_select_fusion.2 = f32[8,448,48]{2,0,1:T(8,128)S(1)} fusion(bf16[24,1,7,99]{0,2,3,1:T(8,128)(2,1)S(1)} %slice.39, bf16[24,1,8,448]{0,2,3,1:T(8,128)(2,1)} %copy-done.1, pred[8,448]{0,1:T(8,128)(4,1)S(1)} %bitcast.61, s32[48]{0:T(128)S(1)} %copy-done.7, bf16[48,100]{0,1:T(8,128)(2,1)S(1)} %copy.96), kind=kOutput, calls=%fused_computation.9.clone.1 | convolution fusion | flops 826786176 | bytes 906800 | tf_op jit(solution)/shard_map/while/body/eval_jaxpr/conv_general_dilated | solution.py:42
  105.2 15.7 %fusion.53 = f32[8,448,24]{2,0,1:T(8,128)} fusion(f32[24,1,7,99]{0,2,3,1:T(8,128)S(1)} %slice.40, f32[24,1,8,448]{0,2,3,1:T(8,128)S(1)} %copy.99), kind=kOutput, calls=%fused_computation.4.clone.1 | convolution fusion | flops 103534272 | bytes 754656 | tf_op jit(solution)/shard_map/while/body/eval_jaxpr/conv_general_dilated | solution.py:24
  120.9 2.1 copy.100
  124.9 47.8 %while.16 = (s32[]{:T(128)}, f32[8,2,3485]{2,1,0:T(2,128)S(1)}, s32[16,3]{0,1:T(4,128)S(1)}, f32[16,3072]{1,0:T(8,128)S(1)}, s32[]{:T(128)}, /*index=5*/s32[]{:T(128)}) while((s32[]{:T(128)}, f32[8,2,3485]{2,1,0:T(2,128)S(1)}, s32[16,3]{0,1:T(4,128)S(1)}, f32[16,3072]{1,0:T(8,128)S(1)}, s32[]{:T(128)}, /*index=5*/s32[]{:T(128)}) %tuple.55), condition=%wide.while_cond, body=%wide.while_body.sunk | while | flops 2 | bytes 49289 | solution.py:57
  128.6 2.0 dynamic-slice_bitcast_fusion.2
  131.6 2.0 dynamic-slice_bitcast_fusion.2
  134.6 2.0 dynamic-slice_bitcast_fusion.2
  140.6 2.0 dynamic-slice_bitcast_fusion.2
  143.5 2.0 dynamic-slice_bitcast_fusion.2
  149.5 2.0 dynamic-slice_bitcast_fusion.2
  152.5 2.0 dynamic-slice_bitcast_fusion.2
  155.5 2.0 dynamic-slice_bitcast_fusion.2
  177.2 9.8 %convolution_select_fusion.2 = f32[8,448,48]{2,0,1:T(8,128)S(1)} fusion(bf16[24,1,7,99]{0,2,3,1:T(8,128)(2,1)S(1)} %slice.39, bf16[24,1,8,448]{0,2,3,1:T(8,128)(2,1)} %copy-done.1, pred[8,448]{0,1:T(8,128)(4,1)S(1)} %bitcast.61, s32[48]{0:T(128)S(1)} %copy-done.7, bf16[48,100]{0,1:T(8,128)(2,1)S(1)} %copy.96), kind=kOutput, calls=%fused_computation.9.clone.1 | convolution fusion | flops 826786176 | bytes 906800 | tf_op jit(solution)/shard_map/while/body/eval_jaxpr/conv_general_dilated | solution.py:42
  189.9 15.7 %fusion.53 = f32[8,448,24]{2,0,1:T(8,128)} fusion(f32[24,1,7,99]{0,2,3,1:T(8,128)S(1)} %slice.40, f32[24,1,8,448]{0,2,3,1:T(8,128)S(1)} %copy.99), kind=kOutput, calls=%fused_computation.4.clone.1 | convolution fusion | flops 103534272 | bytes 754656 | tf_op jit(solution)/shard_map/while/body/eval_jaxpr/conv_general_dilated | solution.py:24
  205.6 2.1 copy.100
  209.6 47.8 %while.16 = (s32[]{:T(128)}, f32[8,2,3485]{2,1,0:T(2,128)S(1)}, s32[16,3]{0,1:T(4,128)S(1)}, f32[16,3072]{1,0:T(8,128)S(1)}, s32[]{:T(128)}, /*index=5*/s32[]{:T(128)}) while((s32[]{:T(128)}, f32[8,2,3485]{2,1,0:T(2,128)S(1)}, s32[16,3]{0,1:T(4,128)S(1)}, f32[16,3072]{1,0:T(8,128)S(1)}, s32[]{:T(128)}, /*index=5*/s32[]{:T(128)}) %tuple.55), condition=%wide.while_cond, body=%wide.while_body.sunk | while | flops 2 | bytes 49289 | solution.py:57
  261.9 9.8 %convolution_select_fusion.2 = f32[8,448,48]{2,0,1:T(8,128)S(1)} fusion(bf16[24,1,7,99]{0,2,3,1:T(8,128)(2,1)S(1)} %slice.39, bf16[24,1,8,448]{0,2,3,1:T(8,128)(2,1)} %copy-done.1, pred[8,448]{0,1:T(8,128)(4,1)S(1)} %bitcast.61, s32[48]{0:T(128)S(1)} %copy-done.7, bf16[48,100]{0,1:T(8,128)(2,1)S(1)} %copy.96), kind=kOutput, calls=%fused_computation.9.clone.1 | convolution fusion | flops 826786176 | bytes 906800 | tf_op jit(solution)/shard_map/while/body/eval_jaxpr/conv_general_dilated | solution.py:42
  274.6 15.7 %fusion.53 = f32[8,448,24]{2,0,1:T(8,128)} fusion(f32[24,1,7,99]{0,2,3,1:T(8,128)S(1)} %slice.40, f32[24,1,8,448]{0,2,3,1:T(8,128)S(1)} %copy.99), kind=kOutput, calls=%fused_computation.4.clone.1 | convolution fusion | flops 103534272 | bytes 754656 | tf_op jit(solution)/shard_map/while/body/eval_jaxpr/conv_general_dilated | solution.py:24
  290.3 2.1 copy.100
  294.3 47.8 %while.16 = (s32[]{:T(128)}, f32[8,2,3485]{2,1,0:T(2,128)S(1)}, s32[16,3]{0,1:T(4,128)S(1)}, f32[16,3072]{1,0:T(8,128)S(1)}, s32[]{:T(128)}, /*index=5*/s32[]{:T(128)}) while((s32[]{:T(128)}, f32[8,2,3485]{2,1,0:T(2,128)S(1)}, s32[16,3]{0,1:T(4,128)S(1)}, f32[16,3072]{1,0:T(8,128)S(1)}, s32[]{:T(128)}, /*index=5*/s32[]{:T(128)}) %tuple.55), condition=%wide.while_cond, body=%wide.while_body.sunk | while | flops 2 | bytes 49289 | solution.py:57
  346.6 9.8 %convolution_select_fusion.2 = f32[8,448,48]{2,0,1:T(8,128)S(1)} fusion(bf16[24,1,7,99]{0,2,3,1:T(8,128)(2,1)S(1)} %slice.39, bf16[24,1,8,448]{0,2,3,1:T(8,128)(2,1)} %copy-done.1, pred[8,448]{0,1:T(8,128)(4,1)S(1)} %bitcast.61, s32[48]{0:T(128)S(1)} %copy-done.7, bf16[48,100]{0,1:T(8,128)(2,1)S(1)} %copy.96), kind=kOutput, calls=%fused_computation.9.clone.1 | convolution fusion | flops 826786176 | bytes 906800 | tf_op jit(solution)/shard_map/while/body/eval_jaxpr/conv_general_dilated | solution.py:42
  359.3 15.7 %fusion.53 = f32[8,448,24]{2,0,1:T(8,128)} fusion(f32[24,1,7,99]{0,2,3,1:T(8,128)S(1)} %slice.40, f32[24,1,8,448]{0,2,3,1:T(8,128)S(1)} %copy.99), kind=kOutput, calls=%fused_computation.4.clone.1 | convolution fusion | flops 103534272 | bytes 754656 | tf_op jit(solution)/shard_map/while/body/eval_jaxpr/conv_general_dilated | solution.py:24
  375.0 2.1 copy.100
  379.0 47.8 %while.16 = (s32[]{:T(128)}, f32[8,2,3485]{2,1,0:T(2,128)S(1)}, s32[16,3]{0,1:T(4,128)S(1)}, f32[16,3072]{1,0:T(8,128)S(1)}, s32[]{:T(128)}, /*index=5*/s32[]{:T(128)}) while((s32[]{:T(128)}, f32[8,2,3485]{2,1,0:T(2,128)S(1)}, s32[16,3]{0,1:T(4,128)S(1)}, f32[16,3072]{1,0:T(8,128)S(1)}, s32[]{:T(128)}, /*index=5*/s32[]{:T(128)}) %tuple.55), condition=%wide.while_cond, body=%wide.while_body.sunk | while | flops 2 | bytes 49289 | solution.py:57
  431.2 9.8 %convolution_select_fusion.2 = f32[8,448,48]{2,0,1:T(8,128)S(1)} fusion(bf16[24,1,7,99]{0,2,3,1:T(8,128)(2,1)S(1)} %slice.39, bf16[24,1,8,448]{0,2,3,1:T(8,128)(2,1)} %copy-done.1, pred[8,448]{0,1:T(8,128)(4,1)S(1)} %bitcast.61, s32[48]{0:T(128)S(1)} %copy-done.7, bf16[48,100]{0,1:T(8,128)(2,1)S(1)} %copy.96), kind=kOutput, calls=%fused_computation.9.clone.1 | convolution fusion | flops 826786176 | bytes 906800 | tf_op jit(solution)/shard_map/while/body/eval_jaxpr/conv_general_dilated | solution.py:42
  444.0 15.7 %fusion.53 = f32[8,448,24]{2,0,1:T(8,128)} fusion(f32[24,1,7,99]{0,2,3,1:T(8,128)S(1)} %slice.40, f32[24,1,8,448]{0,2,3,1:T(8,128)S(1)} %copy.99), kind=kOutput, calls=%fused_computation.4.clone.1 | convolution fusion | flops 103534272 | bytes 754656 | tf_op jit(solution)/shard_map/while/body/eval_jaxpr/conv_general_dilated | solution.py:24
  459.7 2.1 copy.100
  463.7 47.8 %while.16 = (s32[]{:T(128)}, f32[8,2,3485]{2,1,0:T(2,128)S(1)}, s32[16,3]{0,1:T(4,128)S(1)}, f32[16,3072]{1,0:T(8,128)S(1)}, s32[]{:T(128)}, /*index=5*/s32[]{:T(128)}) while((s32[]{:T(128)}, f32[8,2,3485]{2,1,0:T(2,128)S(1)}, s32[16,3]{0,1:T(4,128)S(1)}, f32[16,3072]{1,0:T(8,128)S(1)}, s32[]{:T(128)}, /*index=5*/s32[]{:T(128)}) %tuple.55), condition=%wide.while_cond, body=%wide.while_body.sunk | while | flops 2 | bytes 49289 | solution.py:57
  512.6 12.9 %all-reduce = (f32[2,3072]{1,0:T(2,128)S(1)}, f32[2]{0:T(128)S(1)}) all-reduce(f32[2,3072]{1,0:T(2,128)S(1)} %get-tuple-element.40, f32[2]{0:T(128)S(1)} %convert_element_type.33), channel_id=1, replica_groups=mesh['win'=2,'tmpl'=4,'sta'=4] {'sta'}, use_global_device_ids=true, to_apply=%region_5.6 | all-reduce | flops 6146 | bytes 49168 | tf_op jit(solution)/shard_map/psum | solution.py:103
  525.6 18.9 %pmax.7 = f32[3072]{0:T(1024)S(1)} all-reduce(f32[3072]{0:T(1024)S(1)} %get-tuple-element.140), channel_id=1, replica_groups=mesh['win'=2,'tmpl'=4,'sta'=4] {'tmpl'}, use_global_device_ids=true, to_apply=%region_9.10 | all-reduce | flops 3072 | bytes 24576 | tf_op jit(solution)/shard_map/pmax | solution.py:105
  545.1 16.7 %all-reduce.1 = (f32[3072]{0:T(1024)S(1)}, f32[3,3072]{1,0:T(4,128)S(1)}) all-reduce(f32[3072]{0:T(1024)S(1)} %get-tuple-element.138, f32[3,3072]{1,0:T(4,128)S(1)} %convolution_multiply_fusion), channel_id=1, replica_groups=mesh['win'=2,'tmpl'=4,'sta'=4] {'tmpl'}, use_global_device_ids=true, to_apply=%region_11.12 | all-reduce | flops 12288 | bytes 98304 | tf_op jit(solution)/shard_map/psum | solution.py:107
  (664 shorter events, 299.8 us)
Async XLA Ops:
  0.6 543.9 %copy-start = (f32[3,256]{1,0:T(4,128)S(1)}, f32[3,256]{1,0:T(4,128)}, u32[]{:S(2)}) copy-start(f32[3,256]{1,0:T(4,128)} %param.13) | copy-start | bytes 9220
  3.6 541.0 %copy-start.5 = (s32[2]{0:T(128)S(1)}, s32[2]{0:T(128)}, u32[]{:S(2)}) copy-start(s32[2]{0:T(128)} %param.12) | copy-start | bytes 28
  3.6 4.2 copy-start.6
  3.6 4.2 copy-start.7
  6.8 1.0 copy-start.1
  36.2 2.1 copy-start.3
  38.3 0.8 copy-start.2
  38.7 1.2 copy-start.4
  88.3 4.2 copy-start.6
  88.3 4.2 copy-start.7
  91.5 1.0 copy-start.1
  120.9 2.1 copy-start.3
  123.0 0.8 copy-start.2
  123.4 1.2 copy-start.4
  173.0 4.2 copy-start.6
  173.0 4.2 copy-start.7
  176.2 1.0 copy-start.1
  205.6 2.1 copy-start.3
  207.7 0.8 copy-start.2
  208.1 1.2 copy-start.4
  257.7 4.2 copy-start.6
  257.7 4.2 copy-start.7
  260.9 1.0 copy-start.1
  290.3 2.1 copy-start.3
  292.4 0.8 copy-start.2
  292.8 1.2 copy-start.4
  342.4 4.2 copy-start.6
  342.4 4.2 copy-start.7
  345.6 1.0 copy-start.1
  375.0 2.1 copy-start.3
  377.1 0.8 copy-start.2
  377.5 1.2 copy-start.4
  427.1 4.2 copy-start.6
  427.1 4.2 copy-start.7
  430.3 1.0 copy-start.1
  459.7 2.1 copy-start.3
  461.8 0.8 copy-start.2
  462.2 1.2 copy-start.4
where the time goes:
time: 567 us; the launch traced here: 563 us
  local copies, waits for them, and re-layouts  340 us (60%)
  matrix products  154 us (27%)
  blocking collectives  48.5 us (9%)
  other arithmetic  11.9 us (2%)
  loops' own time  8.41 us (1%)
    gather x384, local copies, waits for them, and re-layouts  284 us
    conv_general_dilated x6, matrix products, window_norm(): lax.conv_general_dilated(squares[None], ones_kernel, (1,), 'VALID', dimen...  94.5 us
    conv_general_dilated x6, matrix products, block_trace(): lax.conv_general_dilated(channels[None], kernel, (1,), 'VALID', dimension...  58.9 us
    pmax x1, blocking collectives, on_device(): best = lax.pmax(best_local, 'tmpl')  18.9 us
    conv_general_dilated x24, local copies, waits for them, and re-layouts, window_norm(): lax.conv_general_dilated(squares[None], ones_kernel, (1,), 'VALID', dimen...  18.7 us
    psum x1, blocking collectives, on_device(): lax.psum((totals * rescale, located * rescale[None, :]), 'tmpl')  16.7 us
    conv_general_dilated x36, local copies, waits for them, and re-layouts, block_trace(): lax.conv_general_dilated(channels[None], kernel, (1,), 'VALID', dimension...  13.1 us
    psum x1, blocking collectives, on_device(): traces, counts = lax.psum((partial_value, own_count), 'sta')  12.9 us

commit v1 on v0

v1 whole, which is shorter than its diff:
```python
import functools
import jax, jax.numpy as jnp
from jax import lax
from jax.experimental import pallas as pl
from jax.experimental.pallas import tpu as pltpu

from jax.sharding import PartitionSpec as P

SAMPLES = 3072
LANES = 128
sharpness = 400.0
epsilon = 1e-06
BIG = 3.0e38

def trace_kernel(group, out_rows, shares, copies, shift_ref, valid_ref, id_ref, rec_ref, tmpl_ref, xyz_ref,
                 out_ref, wav, rows, inv, slot):
    tpls, stas, comps, taps = tmpl_ref.shape
    blocks = rec_ref.shape[-1] // LANES
    pitch = rows.shape[0] // (stas * comps)
    f32 = jnp.float32
    lane = lax.broadcasted_iota(jnp.int32, (LANES, LANES), 1)
    sub = lax.broadcasted_iota(jnp.int32, (LANES, LANES), 0)
    same = lane >= sub

    wav[...] = jnp.zeros(wav.shape, f32)
    for t in range(tpls):
        wide = tmpl_ref[t].astype(f32)
        power = jnp.mean(wide * wide, axis=-1, keepdims=True)
        normed = (wide / (taps * jnp.sqrt(power + epsilon))).astype(jnp.bfloat16).astype(f32)
        wav[t, :, :comps, :taps] = normed

    def spread(s, _):
        wide = rec_ref[s].astype(f32)
        base = s * (comps * pitch)
        for q in range(blocks):
            rows[pl.ds(base + q, comps, stride=pitch), :] = wide[:, q * LANES:(q + 1) * LANES]
        for c in range(comps):
            rows[pl.ds(base + c * pitch + blocks, pitch - blocks), :] = jnp.zeros((pitch - blocks, LANES), f32)
        return _
    lax.fori_loop(0, stas, spread, 0)

    near = (lane < sub + taps) & same
    far = (lane + LANES < sub + taps)
    band = jnp.concatenate([jnp.concatenate([near.astype(f32)] * 2, axis=1),
                            jnp.concatenate([far.astype(f32)] * 2, axis=1)], axis=0).astype(jnp.bfloat16)
    chans = group * comps
    chunk = chans * pitch

    def energy(g, _):
        base = pl.multiple_of(g * chunk, 8)
        wide = rows[pl.ds(base, chunk), :]
        square = jnp.minimum(wide * wide, BIG)
        high = square.astype(jnp.bfloat16)
        low = (square - high.astype(f32)).astype(jnp.bfloat16)
        both = lax.dot_general(jnp.concatenate([high, low], axis=1), band,
                               (((1,), (1,)), ((), ())), preferred_element_type=f32)
        nxt = pltpu.roll(both[:, LANES:], chunk - 1, axis=0)
        inv[pl.ds(base, chunk), :] = lax.rsqrt((both[:, :LANES] + nxt) / taps + epsilon)
        return _
    lax.fori_loop(0, stas // group, energy, 0)

    row_lane = lax.broadcasted_iota(jnp.int32, (out_rows, LANES), 1)

    def step(g, carry):
        accs, counts = list(carry[0]), list(carry[1])
        for u in range(group):
            s = g * group + u
            parts = [None] * tpls
            for c in range(comps):
                base = pl.multiple_of((s * comps + c) * pitch, 8)
                here = rows[pl.ds(base, pitch), :].astype(jnp.bfloat16)
                there = rows[pl.ds(base + 1, pitch), :].astype(jnp.bfloat16)
                left = jnp.concatenate([here, there], axis=1)
                bands = []
                for t in range(tpls):
                    used = valid_ref[t, s, c]
                    counts[t] = counts[t] + used
                    wave = wav[t, s, pl.ds(c, 1), :] * used.astype(f32)
                    ring = pltpu.roll(jnp.broadcast_to(wave, (LANES, LANES)), 0, 1, stride=1, stride_axis=0)
                    bands.append(jnp.concatenate([jnp.where(same, ring, 0.0).astype(jnp.bfloat16),
                                                  jnp.where(same, 0.0, ring).astype(jnp.bfloat16)], axis=1))
                raw = lax.dot_general(left, jnp.concatenate(bands, axis=0), (((1,), (1,)), ((), ())),
                                      preferred_element_type=f32)
                scale = inv[pl.ds(base, pitch), :]
                for t in range(tpls):
                    term = raw[:, t * LANES:(t + 1) * LANES] * scale
                    parts[t] = term if c == 0 else parts[t] + term
            for t in range(tpls):
                shift = shift_ref[t, s]
                skip, turn = shift // LANES, lax.rem(shift, LANES)
                slot[u * tpls + t] = pltpu.roll(parts[t], lax.rem(LANES - turn, LANES), 1)
                first = slot[u * tpls + t, pl.ds(skip, out_rows), :]
                second = slot[u * tpls + t, pl.ds(skip + 1, out_rows), :]
                accs[t] = accs[t] + jnp.where(row_lane < LANES - turn, first, second)
        return tuple(accs), tuple(counts)

    zero = (tuple(jnp.zeros((out_rows, LANES), f32) for _ in range(tpls)), tuple(jnp.int32(0) for _ in range(tpls)))
    accs, counts = lax.fori_loop(0, stas // group, step, zero)

    share = out_rows // shares
    place = lax.broadcasted_iota(jnp.int32, xyz_ref.shape, 1)
    diag = lax.broadcasted_iota(jnp.int32, (xyz_ref.shape[0], LANES), 0) == lax.broadcasted_iota(
        jnp.int32, (xyz_ref.shape[0], LANES), 1)
    for t in range(tpls):
        spot = jnp.sum(jnp.where(place == id_ref[t], xyz_ref[...], 0.0), axis=1, keepdims=True)
        where = jnp.sum(jnp.where(diag, spot, 0.0), axis=0, keepdims=True)
        count = jnp.full((1, LANES), counts[t].astype(f32), f32)
        for b in range(shares):
            for d in range(copies):
                out_ref[d * shares + b, pl.ds(t * share, share), :] = accs[t][b * share:(b + 1) * share]
                out_ref[d * shares + b, pl.ds(tpls * share + t, 1), :] = count
                out_ref[d * shares + b, pl.ds(tpls * share + tpls + t, 1), :] = where


def block_rows(tpls, out_rows, shares):
    need = tpls * (out_rows // shares) + 2 * tpls
    return -(-need // 8) * 8

def traces_call(records, templates, valid, shifts, ids, xyz, out_rows, shares, copies, group=4, interpret=False):
    tpls, stas, comps, taps = templates.shape
    while stas % group: group -= 1
    blocks = records.shape[-1] // LANES
    pitch = -(-(blocks + 1) // 8) * 8
    smem = pl.BlockSpec(memory_space=pltpu.SMEM)
    vmem = pl.BlockSpec(memory_space=pltpu.VMEM)
    return pl.pallas_call(
        functools.partial(trace_kernel, group, out_rows, shares, copies),
        out_shape=jax.ShapeDtypeStruct((copies * shares, block_rows(tpls, out_rows, shares), LANES), jnp.float32),
        in_specs=[smem, smem, smem, vmem, vmem, vmem],
        out_specs=vmem,
        scratch_shapes=[
            pltpu.VMEM((tpls, stas, 8, LANES), jnp.float32),
            pltpu.VMEM((stas * comps * pitch + 8, LANES), jnp.float32),
            pltpu.VMEM((stas * comps * pitch, LANES), jnp.float32),
            pltpu.VMEM((group * tpls, pitch, LANES), jnp.float32),
        ],
        name="traces",
        interpret=interpret,
    )(shifts, valid, ids, records, templates, xyz)


def merge_kernel(shares, tpls, got_ref, peak_ref, evidence_ref, place_ref):
    groups = got_ref.shape[0] // shares
    share = peak_ref.shape[0]
    scores, spots = [], []
    for g in range(groups):
        total = got_ref[g * shares]
        for s in range(1, shares):
            total = total + got_ref[g * shares + s]
        for t in range(tpls):
            trace = total[t * share:(t + 1) * share]
            count = total[tpls * share + t:tpls * share + t + 1]
            scores.append(sharpness * (trace / count))
            row = tpls * share + tpls + t
            spots.append(got_ref[g * shares, row:row + 1, :])
    peak = functools.reduce(jnp.maximum, scores)
    weights = [jnp.exp(score - peak) for score in scores]
    totals = functools.reduce(jnp.add, weights)
    peak_ref[...] = peak
    evidence_ref[...] = peak + jnp.log(totals)
    for j in range(place_ref.shape[0]):
        located = functools.reduce(jnp.add, [w * spot[:, j:j + 1] for w, spot in zip(weights, spots)])
        located = located / totals
        for q in range(share):
            place_ref[j:j + 1, q * LANES:(q + 1) * LANES] = located[q:q + 1]


def on_device(records, templates, channel_valid, shifts, hypo_id, hypo_xyz):
    shares, copies = lax.axis_size("sta"), lax.axis_size("tmpl")
    tpls = templates.shape[0]
    share = SAMPLES // LANES // shares
    sent = traces_call(records, templates, channel_valid, shifts, hypo_id, hypo_xyz, SAMPLES // LANES, shares, copies)
    got = lax.all_to_all(sent, ("tmpl", "sta"), 0, 0, tiled=True)
    flat = jax.ShapeDtypeStruct((share, LANES), jnp.float32)
    vmem = pl.BlockSpec(memory_space=pltpu.VMEM)
    peak, evidence, location = pl.pallas_call(
        functools.partial(merge_kernel, shares, tpls),
        out_shape=(flat, flat, jax.ShapeDtypeStruct((hypo_xyz.shape[0], share * LANES), jnp.float32)),
        in_specs=[vmem],
        out_specs=(vmem, vmem, vmem),
        name="merge",
    )(got)
    return peak.reshape(-1), evidence.reshape(-1), location


def solution(mesh):
    return jax.shard_map(
        on_device,
        mesh=mesh,
        in_specs=(
            P(("win", "sta"), None, None),
            P(("win", "tmpl"), "sta", None, None),
            P(("win", "tmpl"), "sta", None),
            P(("win", "tmpl"), "sta"),
            P(("win", "tmpl")),
            P(),
        ),
        out_specs=(P(("win", "sta")), P(("win", "sta")), P(None, ("win", "sta"))),
        check_vma=False,
    )
```

time: 567 us -> 40.3 us (0.07)
  local copies, waits for them, and re-layouts: 340 us -> 6.14 us
  matrix products: 154 us -> 0 us
  blocking collectives: 48.5 us -> 15.4 us
  Pallas kernels: 0 us -> 17.8 us
  other arithmetic: 11.9 us -> 0 us
  loops' own time: 8.41 us -> 0 us
    gather x402 -> x0, local copies, waits for them, and re-layouts: 286 us -> none
    conv_general_dilated x12 -> x0, matrix products: 153 us -> none  [the longest x6 94.5 us: window_norm(): lax.conv_general_dilated(squares[None], ones_kernel, (1,), 'VALID', dimen...]
    conv_general_dilated x60 -> x0, local copies, waits for them, and re-layouts: 31.8 us -> none  [the longest x24 18.7 us: window_norm(): lax.conv_general_dilated(squares[None], ones_kernel, (1,), 'VALID', dimen...]
    psum x2 -> x0, blocking collectives: 29.6 us -> none  [the longest x1 16.7 us: on_device(): lax.psum((totals * rescale, located * rescale[None, :]), 'tmpl')]
    pmax x1 -> x0, blocking collectives: 18.9 us -> none  [on_device(): best = lax.pmax(best_local, 'tmpl')]
    pallas_call x0 -> x2, Pallas kernels: none -> 17.8 us  [the longest x1 16.2 us: traces_call(): pl.pallas_call(functools.partial(trace_kernel, group, out_rows, shares, c...]
    dynamic_slice x36 -> x0, local copies, waits for them, and re-layouts: 15.5 us -> none  [the longest x12 6.33 us: accumulate(): part_records = lax.dynamic_slice_in_dim(records, first_row, block_size, 0)]
    all_to_all x0 -> x1, blocking collectives: none -> 15.4 us  [on_device(): got = lax.all_to_all(sent, ('tmpl', 'sta'), 0, 0, tiled=True)]
where the time goes in v1:
time: 40.3 us; the launch traced here: 40 us
  Pallas kernels  17.8 us (44%)
  blocking collectives  15.4 us (38%)
  local copies, waits for them, and re-layouts  6.14 us (15%)
  between operations  0.63 us (2%)
    pallas_call x1, Pallas kernels, traces_call(): pl.pallas_call(functools.partial(trace_kernel, group, out_rows, shares, c...  16.2 us
    all_to_all x1, blocking collectives, on_device(): got = lax.all_to_all(sent, ('tmpl', 'sta'), 0, 0, tiled=True)  15.4 us
    unnamed x3, local copies, waits for them, and re-layouts  6.14 us
    pallas_call x1, Pallas kernels, on_device(): pl.pallas_call(functools.partial(merge_kernel, shares, tpls), out_shape=(...  1.63 us

profile of v1, /device:TPU:0, one launch (start us, length us, event | category | flops | bytes accessed | tf_op | source)
XLA Modules:
  0.0 40.0 jit_solution(7684452442163089119)
XLA Ops:
  0.6 1.4 %copy.9.valid_ref = s32[2,48,3]{2,1,0:T(8,128)} copy(s32[2,48,3]{1,0,2:T(2,128)} %param.8) | data formatting | bytes 2304 | tf_op args[2]
  2.0 1.5 %copy.11.tmpl_ref = bf16[2,48,3,100]{3,2,1,0:T(4,128)(2,1)} copy(bf16[2,48,3,100]{3,1,2,0:T(8,128)(2,1)} %param.7) | data formatting | bytes 115200 | tf_op args[1]
  3.6 3.2 %copy.10.rec_ref = bf16[48,3,3584]{2,1,0:T(4,128)(2,1)} copy(bf16[48,3,3584]{2,0,1:T(8,128)(2,1)} %param.6) | data formatting | bytes 2064384 | tf_op args[0]
  6.8 16.2 %traces.1 = f32[16,16,128]{2,1,0:T(8,128)} custom-call(s32[2,48]{1,0:T(2,128)} %shift_ref.1, s32[2,48,3]{2,1,0:T(8,128)} %copy.9.valid_ref, s32[2]{0:T(128)} %id_ref.1, bf16[48,3,3584]{2,1,0:T(4,128)(2,1)} %copy.10.rec_ref, bf16[2,48,3,100]{3,2,1,0:T(4,128)(2,1)} %copy.11.tmpl_ref, f32[3,256]{1,0:T(4,128)} %xyz_ref.1), custom_call_target="tpu_custom_call" | custom-call | tf_op jit(solution)/shard_map/traces/pallas_call | solution.py:126
  22.9 15.4 %all_to_all.5.got_ref = f32[16,16,128]{2,1,0:T(8,128)} all-to-all(f32[16,16,128]{2,1,0:T(8,128)} %traces.1), channel_id=1, replica_groups=mesh['win'=2,'tmpl'=4,'sta'=4] {'tmpl','sta'}, dimensions={0} | all-to-all | bytes 262144 | tf_op jit(solution)/shard_map/all_to_all | solution.py:173
  38.3 1.6 %merge.1 = (f32[6,128]{1,0:T(8,128)}, f32[6,128]{1,0:T(8,128)}, f32[3,768]{1,0:T(4,128)}) custom-call(f32[16,16,128]{2,1,0:T(8,128)} %all_to_all.5.got_ref), custom_call_target="tpu_custom_call" | custom-call | tf_op jit(solution)/shard_map/merge/pallas_call | solution.py:176
